TPU v7x, 32 devices: a whole 2x2x4 slice. The times are simulated.
32 devices in a mesh: dp: 4 (over z), seq: 8 (over y, x, core).
Axes of the slice: x: 2, y: 2, z: 4, core: 2. Of those that a mesh axis runs over, the one named last changes fastest.
Arguments:
- tokens: float32 [4, 1024, 2048], P('dp', 'seq'), may hold values from -10 to 10, as said below
- cotangent: float32 [4, 1024, 2048], P('dp', 'seq'), may hold values from -6 to 6
- short_weights: float32 [3, 8, 2048], replicated, may hold values from 0.2 to 0.6
Outputs:
- grad_tokens: float32 [4, 1024, 2048], P('dp', 'seq')
- grad_weights: float32 [3, 8, 2048], P(None, None, 'seq')
Inputs may be any that keep to these rules, and one draw needn't show every extreme that they name: `tokens`: Real-valued activations of order one.
All inputs are finite; a program needn't handle non-finite values.
Results may differ from a plain program's by a relative error of at most 0.0003.
Values sent between devices are 32-bit elements; how exact they have to be, the bound alone decides.
No kernel may reach another device: no remote copies, remote signals or barrier semaphores. Data moves between devices by JAX's collectives and lax.ppermute only.
A program may use at most 64 MiB of HBM per device.

v0:
```python
import jax
import jax.numpy as jnp
from jax import lax
from jax.sharding import PartitionSpec as P

HEAD = 64
D = 2048
K = 8


def attend_back(query, key, value, grad_o):
    scale = HEAD ** (-0.5)
    hi = lax.Precision.HIGHEST
    scores = scale * jnp.einsum("qhe,khe->hqk", query, key, precision=hi)
    top = jnp.max(scores, axis=-1, keepdims=True)
    expo = jnp.exp(scores - top)
    probs = expo / jnp.sum(expo, axis=-1, keepdims=True)
    grad_probs = jnp.einsum("qhe,khe->hqk", grad_o, value, precision=hi)
    delta = jnp.sum(probs * grad_probs, axis=-1, keepdims=True)
    grad_scores = probs * (grad_probs - delta)
    grad_q = scale * jnp.einsum("hqk,khe->qhe", grad_scores, key, precision=hi)
    grad_k = scale * jnp.einsum("hqk,qhe->khe", grad_scores, query, precision=hi)
    grad_v = jnp.einsum("hqk,qhe->khe", probs, grad_o, precision=hi)
    return (grad_q, grad_k, grad_v)


def head_backward(query, key, value, grad_o):
    batch, sums, width = query.shape
    heads_here = width // HEAD

    def one_sequence(parts):
        shaped = [p.reshape(sums, heads_here, HEAD) for p in parts]
        grads = attend_back(shaped[0], shaped[1], shaped[2], shaped[3])
        return tuple((g.reshape(sums, width) for g in grads))

    return jax.vmap(one_sequence)((query, key, value, grad_o))


def per_device(tokens, cotangent, short_weights):
    hi = lax.Precision.HIGHEST
    batch = tokens.shape[0]
    col_tokens, col_grad = (
        lax.all_to_all(tokens, "seq", split_axis=2, concat_axis=1, tiled=True),
        lax.all_to_all(cotangent, "seq", split_axis=2, concat_axis=1, tiled=True),
    )
    length = col_tokens.shape[1]
    width = col_tokens.shape[2]
    sums = length // K
    start = lax.axis_index("seq") * width
    local_weights = lax.dynamic_slice_in_dim(short_weights, start, width, 2)
    grouped = col_tokens.reshape(batch, sums, K, width)
    summary = jnp.einsum("bjic,mic->mbjc", grouped, local_weights, precision=hi)
    grad_o = jnp.sum(col_grad.reshape(batch, sums, K, width), axis=2)
    grad_q, grad_k, grad_v = head_backward(summary[0], summary[1], summary[2], grad_o)
    grad_summary = jnp.stack([grad_q, grad_k, grad_v])
    grad_cols = jnp.einsum("mbjc,mic->bjic", grad_summary, local_weights, precision=hi).reshape(
        batch, length, width
    )
    grad_tokens = lax.all_to_all(grad_cols, "seq", split_axis=1, concat_axis=2, tiled=True)
    partial_value = jnp.einsum("mbjc,bjic->mic", grad_summary, grouped, precision=hi)
    raw = lax.psum(partial_value, "dp")
    total_sq = lax.psum(jnp.sum(raw * raw), "seq")
    mean_sq = total_sq / (3 * K * D)
    factor = jnp.minimum(1.0, 1.0 / jnp.sqrt(mean_sq + 1e-06))
    return (grad_tokens, raw * factor)


def solution(mesh):
    return jax.shard_map(
        per_device,
        mesh=mesh,
        in_specs=(P("dp", "seq", None), P("dp", "seq", None), P()),
        out_specs=(P("dp", "seq", None), P(None, None, "seq")),
        check_vma=False,
    )
```

profile of v0, /device:TPU:0, one launch (start us, length us, event | category | flops | bytes accessed | tf_op | source)
XLA Modules:
  0.0 110.5 jit_solution(7120607152902859944)
XLA Ops:
  0.6 3.6 %copy.65 = f32[1,128,2048]{1,0,2:T(1,128)} copy(f32[1,128,2048]{2,1,0:T(8,128)} %param.4) | data formatting | bytes 2097152 | tf_op args[1]
  4.3 5.3 %all-to-all-start.1 = ((f32[1,128,2048]{1,0,2:T(1,128)}), f32[1,128,2048]{1,0,2:T(1,128)S(1)}, u32[]{:S(2)}, u32[]{:S(2)}) async-start(f32[1,128,2048]{1,0,2:T(1,128)} %copy.65), calls=%async_computation.1 | async-start | bytes 2097152 | tf_op jit(solution)/shard_map/all_to_all | solution.py:44
  9.6 1.9 %copy.62 = f32[1,128,2048]{1,0,2:T(1,128)} copy(f32[1,128,2048]{2,1,0:T(8,128)S(1)} %copy-done.1) | data formatting | bytes 2097152 | tf_op args[0]
  11.5 13.5 %all-to-all-done.1 = f32[1,128,2048]{1,0,2:T(1,128)S(1)} async-done(((f32[1,128,2048]{1,0,2:T(1,128)}), f32[1,128,2048]{1,0,2:T(1,128)S(1)}, u32[]{:S(2)}, u32[]{:S(2)}) %all-to-all-start.1) | async-done | bytes 1048608 | tf_op jit(solution)/shard_map/all_to_all | solution.py:44
  25.0 3.6 %all-to-all-start = ((f32[1,128,2048]{1,0,2:T(1,128)}), f32[1,128,2048]{1,0,2:T(1,128)S(1)}, u32[]{:S(2)}, u32[]{:S(2)}) async-start(f32[1,128,2048]{1,0,2:T(1,128)} %copy.62), calls=%async_computation | async-start | bytes 2097152 | tf_op jit(solution)/shard_map/all_to_all | solution.py:43
  28.8 1.3 %copy.66 = f32[1,8,128,256]{3,2,1,0:T(8,128)} copy(f32[1,8,128,256]{2,3,1,0:T(8,128)S(1)} %bitcast.64) | data formatting | bytes 2097152 | tf_op jit(solution)/shard_map/all_to_all | solution.py:44
  30.1 1.5 %reduce_sum.37 = f32[128,256]{1,0:T(8,128)S(1)} reduce(f32[128,8,256]{2,1,0:T(8,128)} %bitcast.65, f32[]{:T(128)} %constant.6.clone.1), dimensions={1}, to_apply=%region_2.0 | reduce | flops 229376 | bytes 1179652 | tf_op jit(solution)/shard_map/reduce_sum | solution.py:53
  31.7 12.2 %all-to-all-done = f32[1,128,2048]{1,0,2:T(1,128)S(1)} async-done(((f32[1,128,2048]{1,0,2:T(1,128)}), f32[1,128,2048]{1,0,2:T(1,128)S(1)}, u32[]{:S(2)}, u32[]{:S(2)}) %all-to-all-start) | async-done | bytes 1048608 | tf_op jit(solution)/shard_map/all_to_all | solution.py:43
  44.2 0.6 copy.64
  44.8 1.8 %convolution_bitcast_fusion.2 = f32[3,1,128,256]{2,0,3,1:T(4,128)S(1)} fusion(f32[3,8,256]{1,0,2:T(4,128)S(1)} %copy.84, f32[128,8,256]{0,1,2:T(8,128)S(1)} %copy.64), kind=kOutput, calls=%fused_computation.2 | convolution fusion | flops 9437184 | bytes 1466368 | tf_op jit(solution)/shard_map/bjic,mic->mbjc/dot_general | solution.py:52
  46.8 0.6 fusion.9
  47.5 0.6 fusion.5
  48.1 0.6 multiply_reduce_fusion.1
  48.7 0.6 convolution_multiply_fusion.1
  50.4 3.4 %convolution_bitcast_fusion = f32[1,128,8,256]{1,2,3,0:T(8,128)} fusion(f32[3,8,256]{1,0,2:T(4,128)S(1)} %copy.84, f32[1,1,128,256]{2,0,3,1:T(1,128)S(1)} %bitcast.74, f32[1,1,128,256]{2,0,3,1:T(1,128)S(1)} %bitcast.76, f32[1,1,128,256]{2,0,3,1:T(1,128)S(1)} %bitcast.78), kind=kOutput, calls=%fused_computation | convolution fusion | flops 9633792 | bytes 1466368 | tf_op jit(solution)/shard_map/mbjc,mic->bjic/dot_general | solution.py:56
  53.8 1.7 %copy.74 = f32[1,128,8,256]{3,2,1,0:T(8,128)S(1)} copy(f32[1,128,8,256]{1,2,3,0:T(8,128)} %convolution_bitcast_fusion) | data formatting | bytes 2097152 | tf_op jit(solution)/shard_map/mbjc,mic->bjic/transpose | solution.py:56
  55.6 2.0 %copy.75 = f32[1,1024,256]{2,0,1:T(1,128)} copy(f32[1,1024,256]{2,1,0:T(8,128)S(1)} %bitcast.67) | data formatting | bytes 2097152 | tf_op jit(solution)/shard_map/reshape | solution.py:56
  57.6 3.9 %all-to-all-start.2 = ((f32[1,1024,256]{2,0,1:T(1,128)}), f32[1,1024,256]{2,0,1:T(1,128)S(1)}, u32[]{:S(2)}, u32[]{:S(2)}) async-start(f32[1,1024,256]{2,0,1:T(1,128)} %copy.75), calls=%async_computation.2 | async-start | bytes 2097152 | tf_op jit(solution)/shard_map/all_to_all | solution.py:59
  61.5 2.0 %convolution_bitcast_fusion.1 = f32[3,8,256]{1,0,2:T(4,128)S(1)} fusion(f32[128,8,256]{0,1,2:T(8,128)S(1)} %copy.64, f32[1,1,128,256]{2,0,3,1:T(1,128)S(1)} %bitcast.75, f32[1,1,128,256]{2,0,3,1:T(1,128)S(1)} %bitcast.77, f32[1,1,128,256]{2,0,3,1:T(1,128)S(1)} %bitcast.79), kind=kOutput, calls=%fused_computation.1 | convolution fusion | flops 9633792 | bytes 1466368 | tf_op jit(solution)/shard_map/mbjc,bjic->mic/dot_general | solution.py:60
  63.5 30.4 %psum.14 = f32[3,8,256]{1,0,2:T(4,128)S(1)} all-reduce(f32[3,8,256]{1,0,2:T(4,128)S(1)} %convolution_bitcast_fusion.1), channel_id=1, replica_groups=mesh['dp'=4,'seq'=8] {'dp'}, use_global_device_ids=true, to_apply=%region_4.0 | all-reduce | flops 6144 | bytes 49152 | tf_op jit(solution)/shard_map/psum | solution.py:61
  94.0 0.9 multiply_reduce_fusion
  94.8 12.4 %psum.15 = f32[]{:T(128)} all-reduce(f32[]{:T(128)} %multiply_reduce_fusion), channel_id=1, replica_groups=mesh['dp'=4,'seq'=8] {'seq'}, use_global_device_ids=true, to_apply=%region_6.0 | all-reduce | flops 1 | bytes 8 | tf_op jit(solution)/shard_map/psum | solution.py:62
  108.0 0.8 copy.79
  109.2 1.3 %copy.78 = f32[1,128,2048]{2,1,0:T(8,128)} copy(f32[1,128,2048]{1,2,0:T(8,128)S(1)} %bitcast.69) | data formatting | bytes 2097152
  (23 shorter events, 2.6 us)
Async XLA Ops:
  0.6 27.9 %copy-start = (f32[3,8,2048]{2,1,0:T(8,128)S(1)}, f32[3,8,2048]{2,1,0:T(8,128)}, u32[]{:S(2)}) copy-start(f32[3,8,2048]{2,1,0:T(8,128)} %param.5) | copy-start | bytes 589828
  4.3 5.3 %copy-start.1 = (f32[1,128,2048]{2,1,0:T(8,128)S(1)}, f32[1,128,2048]{2,1,0:T(8,128)}, u32[]{:S(2)}) copy-start(f32[1,128,2048]{2,1,0:T(8,128)} %param.3) | copy-start | bytes 3145732
  4.3 20.7 %all-to-all-start.1 = ((f32[1,128,2048]{1,0,2:T(1,128)}), f32[1,128,2048]{1,0,2:T(1,128)S(1)}, u32[]{:S(2)}, u32[]{:S(2)}) async-start(f32[1,128,2048]{1,0,2:T(1,128)} %copy.65), calls=%async_computation.1 | async-start | bytes 2097152 | tf_op jit(solution)/shard_map/all_to_all | solution.py:44
  25.0 18.9 %all-to-all-start = ((f32[1,128,2048]{1,0,2:T(1,128)}), f32[1,128,2048]{1,0,2:T(1,128)S(1)}, u32[]{:S(2)}, u32[]{:S(2)}) async-start(f32[1,128,2048]{1,0,2:T(1,128)} %copy.62), calls=%async_computation | async-start | bytes 2097152 | tf_op jit(solution)/shard_map/all_to_all | solution.py:43
  49.4 0.6 copy-start.2
  49.8 0.7 copy-start.4
  57.6 3.9 %copy-start.3 = (f32[4,64,128]{2,1,0:T(8,128)S(1)}, f32[4,64,128]{2,1,0:T(8,128)}, u32[]{:S(2)}) copy-start(f32[4,64,128]{2,1,0:T(8,128)} %copy-done.2) | copy-start | bytes 393220
  57.6 3.9 %copy-start.5 = (f32[4,64,128]{2,1,0:T(8,128)S(1)}, f32[4,64,128]{2,1,0:T(8,128)}, u32[]{:S(2)}) copy-start(f32[4,64,128]{2,1,0:T(8,128)} %copy-done.4) | copy-start | bytes 393220
  57.6 51.2 %all-to-all-start.2 = ((f32[1,1024,256]{2,0,1:T(1,128)}), f32[1,1024,256]{2,0,1:T(1,128)S(1)}, u32[]{:S(2)}, u32[]{:S(2)}) async-start(f32[1,1024,256]{2,0,1:T(1,128)} %copy.75), calls=%async_computation.2 | async-start | bytes 2097152 | tf_op jit(solution)/shard_map/all_to_all | solution.py:59
where the time goes:
time: 111 us
  blocking collectives  42.8 us (39%)
  waiting for transfers between devices  25.6 us (23%)
  local copies, waits for them, and re-layouts  15.2 us (14%)
  starting transfers between devices  12.8 us (12%)
  matrix products  10 us (9%)
  other arithmetic  2.51 us (2%)
  between operations  1.53 us (1%)
    psum x1, blocking collectives, per_device(): raw = lax.psum(partial_value, 'dp')  30.4 us
    all_to_all x1, waiting for transfers between devices, per_device(): lax.all_to_all(cotangent, 'seq', split_axis=2, concat_axis=1, tiled=True)  13.5 us
    psum x1, blocking collectives, per_device(): total_sq = lax.psum(jnp.sum(raw * raw), 'seq')  12.4 us
    all_to_all x1, waiting for transfers between devices, per_device(): lax.all_to_all(tokens, 'seq', split_axis=2, concat_axis=1, tiled=True)  12.2 us
    unnamed x18, local copies, waits for them, and re-layouts  8.56 us
    all_to_all x1, starting transfers between devices, per_device(): lax.all_to_all(cotangent, 'seq', split_axis=2, concat_axis=1, tiled=True)  5.33 us
    all_to_all x1, starting transfers between devices, per_device(): lax.all_to_all(grad_cols, 'seq', split_axis=1, concat_axis=2, tiled=True)  3.87 us
    all_to_all x1, starting transfers between devices, per_device(): lax.all_to_all(tokens, 'seq', split_axis=2, concat_axis=1, tiled=True)  3.56 us
  transfers between devices with their start and end apart: 3, of which 2 were waited for; matrix products, arithmetic and copies ran while one was open for 8% of the time, Pallas kernels for 0%

commit v1 on v0

--- a/solution.py
+++ b/solution.py
@@ -58,7 +58,9 @@
     )
     grad_tokens = lax.all_to_all(grad_cols, "seq", split_axis=1, concat_axis=2, tiled=True)
     partial_value = jnp.einsum("mbjc,bjic->mic", grad_summary, grouped, precision=hi)
-    raw = lax.psum(partial_value, "dp")
+    raw = partial_value
+    for hop in (1, 2):
+        raw = raw + lax.ppermute(raw, "dp", [(dev, dev ^ hop) for dev in range(4)])
     total_sq = lax.psum(jnp.sum(raw * raw), "seq")
     mean_sq = total_sq / (3 * K * D)
     factor = jnp.minimum(1.0, 1.0 / jnp.sqrt(mean_sq + 1e-06))

time: 111 us -> 120 us (1.081)
  waiting for transfers between devices: 25.6 us -> 60.9 us
  blocking collectives: 42.8 us -> 13.5 us
  starting transfers between devices: 12.8 us -> 16.9 us
    ppermute x0 -> x2, waiting for transfers between devices: none -> 35.2 us  [per_device(): raw = raw + lax.ppermute(raw, 'dp', [(dev, dev ^ hop) for dev in range(4)])]
    psum x1 -> x0, blocking collectives: 30.4 us -> none  [per_device(): raw = lax.psum(partial_value, 'dp')]
    ppermute x0 -> x2, starting transfers between devices: none -> 4.29 us  [per_device(): raw = raw + lax.ppermute(raw, 'dp', [(dev, dev ^ hop) for dev in range(4)])]
    unnamed x18 -> x10, local copies, waits for them, and re-layouts: 8.56 us -> 7.91 us
  transfers between devices with their start and end apart: 3 -> 5, of which waited for: 2 -> 4; matrix products, arithmetic and copies ran while one was open for 8% -> 7% of each run, Pallas kernels for 0% -> 0%
where the time goes in v1:
time: 120 us
  waiting for transfers between devices  60.9 us (51%)
  starting transfers between devices  16.9 us (14%)
  local copies, waits for them, and re-layouts  14.6 us (12%)
  blocking collectives  13.5 us (11%)
  matrix products  10 us (8%)
  other arithmetic  2.65 us (2%)
  between operations  1.49 us (1%)
    ppermute x2, waiting for transfers between devices, per_device(): raw = raw + lax.ppermute(raw, 'dp', [(dev, dev ^ hop) for dev in range(4)])  35.2 us
    psum x1, blocking collectives, per_device(): total_sq = lax.psum(jnp.sum(raw * raw), 'seq')  13.5 us
    all_to_all x1, waiting for transfers between devices, per_device(): lax.all_to_all(cotangent, 'seq', split_axis=2, concat_axis=1, tiled=True)  13.5 us
    all_to_all x1, waiting for transfers between devices, per_device(): lax.all_to_all(tokens, 'seq', split_axis=2, concat_axis=1, tiled=True)  12.2 us
    unnamed x10, local copies, waits for them, and re-layouts  7.91 us
    all_to_all x1, starting transfers between devices, per_device(): lax.all_to_all(cotangent, 'seq', split_axis=2, concat_axis=1, tiled=True)  5.33 us
    ppermute x2, starting transfers between devices, per_device(): raw = raw + lax.ppermute(raw, 'dp', [(dev, dev ^ hop) for dev in range(4)])  4.29 us
    all_to_all x1, starting transfers between devices, per_device(): lax.all_to_all(grad_cols, 'seq', split_axis=1, concat_axis=2, tiled=True)  3.74 us
  transfers between devices with their start and end apart: 5, of which 4 were waited for; matrix products, arithmetic and copies ran while one was open for 7% of the time, Pallas kernels for 0%

profile of v1, /device:TPU:0, one launch (start us, length us, event | category | flops | bytes accessed | tf_op | source)
XLA Modules:
  0.0 120.0 jit_solution(6242271097735200544)
XLA Ops:
  0.6 3.6 %copy.65 = f32[1,128,2048]{1,0,2:T(1,128)} copy(f32[1,128,2048]{2,1,0:T(8,128)} %param.4) | data formatting | bytes 2097152 | tf_op args[1]
  4.3 5.3 %all-to-all-start.1 = ((f32[1,128,2048]{1,0,2:T(1,128)}), f32[1,128,2048]{1,0,2:T(1,128)S(1)}, u32[]{:S(2)}, u32[]{:S(2)}) async-start(f32[1,128,2048]{1,0,2:T(1,128)} %copy.65), calls=%async_computation.1 | async-start | bytes 2097152 | tf_op jit(solution)/shard_map/all_to_all | solution.py:44
  9.6 1.9 %copy.62 = f32[1,128,2048]{1,0,2:T(1,128)} copy(f32[1,128,2048]{2,1,0:T(8,128)S(1)} %copy-done.1) | data formatting | bytes 2097152 | tf_op args[0]
  11.5 13.5 %all-to-all-done.1 = f32[1,128,2048]{1,0,2:T(1,128)S(1)} async-done(((f32[1,128,2048]{1,0,2:T(1,128)}), f32[1,128,2048]{1,0,2:T(1,128)S(1)}, u32[]{:S(2)}, u32[]{:S(2)}) %all-to-all-start.1) | async-done | bytes 1048608 | tf_op jit(solution)/shard_map/all_to_all | solution.py:44
  25.0 3.6 %all-to-all-start = ((f32[1,128,2048]{1,0,2:T(1,128)}), f32[1,128,2048]{1,0,2:T(1,128)S(1)}, u32[]{:S(2)}, u32[]{:S(2)}) async-start(f32[1,128,2048]{1,0,2:T(1,128)} %copy.62), calls=%async_computation | async-start | bytes 2097152 | tf_op jit(solution)/shard_map/all_to_all | solution.py:43
  28.8 1.3 %copy.66 = f32[1,8,128,256]{3,2,1,0:T(8,128)} copy(f32[1,8,128,256]{2,3,1,0:T(8,128)S(1)} %bitcast.64) | data formatting | bytes 2097152 | tf_op jit(solution)/shard_map/all_to_all | solution.py:44
  30.1 1.5 %reduce_sum.37 = f32[128,256]{1,0:T(8,128)S(1)} reduce(f32[128,8,256]{2,1,0:T(8,128)} %bitcast.65, f32[]{:T(128)} %constant.6.clone.1), dimensions={1}, to_apply=%region_2.0 | reduce | flops 229376 | bytes 1179652 | tf_op jit(solution)/shard_map/reduce_sum | solution.py:53
  31.7 12.2 %all-to-all-done = f32[1,128,2048]{1,0,2:T(1,128)S(1)} async-done(((f32[1,128,2048]{1,0,2:T(1,128)}), f32[1,128,2048]{1,0,2:T(1,128)S(1)}, u32[]{:S(2)}, u32[]{:S(2)}) %all-to-all-start) | async-done | bytes 1048608 | tf_op jit(solution)/shard_map/all_to_all | solution.py:43
  44.8 1.8 %convolution_bitcast_fusion.2 = f32[3,1,128,256]{2,0,3,1:T(4,128)S(1)} fusion(f32[3,8,256]{1,0,2:T(4,128)S(1)} %copy.84, f32[128,8,256]{0,1,2:T(8,128)S(1)} %copy.64), kind=kOutput, calls=%fused_computation.2 | convolution fusion | flops 9437184 | bytes 1466368 | tf_op jit(solution)/shard_map/bjic,mic->mbjc/dot_general | solution.py:52
  48.1 0.6 multiply_reduce_fusion.1
  48.7 0.6 convolution_multiply_fusion.1
  49.8 3.4 %convolution_bitcast_fusion = f32[1,128,8,256]{1,2,3,0:T(8,128)} fusion(f32[3,8,256]{1,0,2:T(4,128)S(1)} %copy.84, f32[1,1,128,256]{2,0,3,1:T(1,128)S(1)} %bitcast.74, f32[1,1,128,256]{2,0,3,1:T(1,128)S(1)} %bitcast.76, f32[1,1,128,256]{2,0,3,1:T(1,128)S(1)} %bitcast.78), kind=kOutput, calls=%fused_computation | convolution fusion | flops 9633792 | bytes 1466368 | tf_op jit(solution)/shard_map/mbjc,mic->bjic/dot_general | solution.py:56
  53.2 1.7 %copy.74 = f32[1,128,8,256]{3,2,1,0:T(8,128)S(1)} copy(f32[1,128,8,256]{1,2,3,0:T(8,128)} %convolution_bitcast_fusion) | data formatting | bytes 2097152 | tf_op jit(solution)/shard_map/mbjc,mic->bjic/transpose | solution.py:56
  54.9 2.0 %copy.75 = f32[1,1024,256]{2,0,1:T(1,128)} copy(f32[1,1024,256]{2,1,0:T(8,128)S(1)} %bitcast.67) | data formatting | bytes 2097152 | tf_op jit(solution)/shard_map/reshape | solution.py:56
  57.0 3.7 %all-to-all-start.2 = ((f32[1,1024,256]{2,0,1:T(1,128)}), f32[1,1024,256]{2,0,1:T(1,128)S(1)}, u32[]{:S(2)}, u32[]{:S(2)}) async-start(f32[1,1024,256]{2,0,1:T(1,128)} %copy.75), calls=%async_computation.2 | async-start | bytes 2097152 | tf_op jit(solution)/shard_map/all_to_all | solution.py:59
  60.7 2.0 %convolution_bitcast_fusion.1 = f32[3,8,256]{1,0,2:T(4,128)S(1)} fusion(f32[128,8,256]{0,1,2:T(8,128)S(1)} %copy.64, f32[1,1,128,256]{2,0,3,1:T(1,128)S(1)} %bitcast.75, f32[1,1,128,256]{2,0,3,1:T(1,128)S(1)} %bitcast.77, f32[1,1,128,256]{2,0,3,1:T(1,128)S(1)} %bitcast.79), kind=kOutput, calls=%fused_computation.1 | convolution fusion | flops 9633792 | bytes 1466368 | tf_op jit(solution)/shard_map/mbjc,bjic->mic/dot_general | solution.py:60
  62.7 1.6 %collective-permute-start = (f32[3,8,256]{1,0,2:T(4,128)S(1)}, f32[3,8,256]{1,0,2:T(4,128)S(1)}, u32[]{:S(2)}, u32[]{:S(2)}) collective-permute-start(f32[3,8,256]{1,0,2:T(4,128)S(1)} %convolution_bitcast_fusion.1), channel_id=1, source_target_pairs={{0,8},{8,0},{16,24},{24,16},{1,9},{9,1},{17,25},{25,17},{2,10},{10... | collective-permute-start | bytes 73736 | tf_op jit(solution)/shard_map/ppermute | solution.py:63
  64.4 12.5 %collective-permute-done = f32[3,8,256]{1,0,2:T(4,128)S(1)} collective-permute-done((f32[3,8,256]{1,0,2:T(4,128)S(1)}, f32[3,8,256]{1,0,2:T(4,128)S(1)}, u32[]{:S(2)}, u32[]{:S(2)}) %collective-permute-start) | collective-permute-done | bytes 24608 | tf_op jit(solution)/shard_map/ppermute | solution.py:63
  77.0 2.7 %collective-permute-start.1 = (f32[3,8,256]{1,0,2:T(4,128)S(1)}, f32[3,8,256]{1,0,2:T(4,128)S(1)}, u32[]{:S(2)}, u32[]{:S(2)}) collective-permute-start(f32[3,8,256]{1,0,2:T(4,128)S(1)} %add.15), channel_id=1, source_target_pairs={{0,16},{8,24},{16,0},{24,8},{1,17},{9,25},{17,1},{25,9},{2,18},{10... | collective-permute-start | bytes 73736 | tf_op jit(solution)/shard_map/ppermute | solution.py:63
  79.7 22.7 %collective-permute-done.1 = f32[3,8,256]{1,0,2:T(4,128)S(1)} collective-permute-done((f32[3,8,256]{1,0,2:T(4,128)S(1)}, f32[3,8,256]{1,0,2:T(4,128)S(1)}, u32[]{:S(2)}, u32[]{:S(2)}) %collective-permute-start.1) | collective-permute-done | bytes 24608 | tf_op jit(solution)/shard_map/ppermute | solution.py:63
  102.4 0.9 multiply_reduce_fusion
  103.3 13.5 %psum.7 = f32[]{:T(128)} all-reduce(f32[]{:T(128)} %get-tuple-element.12), channel_id=1, replica_groups=mesh['dp'=4,'seq'=8] {'seq'}, use_global_device_ids=true, to_apply=%region_5.0 | all-reduce | flops 1 | bytes 8 | tf_op jit(solution)/shard_map/psum | solution.py:64
  117.5 0.8 copy.79
  118.7 1.3 %copy.78 = f32[1,128,2048]{2,1,0:T(8,128)} copy(f32[1,128,2048]{1,2,0:T(8,128)S(1)} %bitcast.69) | data formatting | bytes 2097152
  (19 shorter events, 3.8 us)
Async XLA Ops:
  0.6 27.9 %copy-start = (f32[3,8,2048]{2,1,0:T(8,128)S(1)}, f32[3,8,2048]{2,1,0:T(8,128)}, u32[]{:S(2)}) copy-start(f32[3,8,2048]{2,1,0:T(8,128)} %param.5) | copy-start | bytes 589828
  4.3 5.3 %copy-start.1 = (f32[1,128,2048]{2,1,0:T(8,128)S(1)}, f32[1,128,2048]{2,1,0:T(8,128)}, u32[]{:S(2)}) copy-start(f32[1,128,2048]{2,1,0:T(8,128)} %param.3) | copy-start | bytes 3145732
  4.3 20.7 %all-to-all-start.1 = ((f32[1,128,2048]{1,0,2:T(1,128)}), f32[1,128,2048]{1,0,2:T(1,128)S(1)}, u32[]{:S(2)}, u32[]{:S(2)}) async-start(f32[1,128,2048]{1,0,2:T(1,128)} %copy.65), calls=%async_computation.1 | async-start | bytes 2097152 | tf_op jit(solution)/shard_map/all_to_all | solution.py:44
  25.0 18.9 %all-to-all-start = ((f32[1,128,2048]{1,0,2:T(1,128)}), f32[1,128,2048]{1,0,2:T(1,128)S(1)}, u32[]{:S(2)}, u32[]{:S(2)}) async-start(f32[1,128,2048]{1,0,2:T(1,128)} %copy.62), calls=%async_computation | async-start | bytes 2097152 | tf_op jit(solution)/shard_map/all_to_all | solution.py:43
  57.0 61.3 %all-to-all-start.2 = ((f32[1,1024,256]{2,0,1:T(1,128)}), f32[1,1024,256]{2,0,1:T(1,128)S(1)}, u32[]{:S(2)}, u32[]{:S(2)}) async-start(f32[1,1024,256]{2,0,1:T(1,128)} %copy.75), calls=%async_computation.2 | async-start | bytes 2097152 | tf_op jit(solution)/shard_map/all_to_all | solution.py:59
  62.7 14.1 %collective-permute-start = (f32[3,8,256]{1,0,2:T(4,128)S(1)}, f32[3,8,256]{1,0,2:T(4,128)S(1)}, u32[]{:S(2)}, u32[]{:S(2)}) collective-permute-start(f32[3,8,256]{1,0,2:T(4,128)S(1)} %convolution_bitcast_fusion.1), channel_id=1, source_target_pairs={{0,8},{8,0},{16,24},{24,16},{1,9},{9,1},{17,25},{25,17},{2,10},{10... | collective-permute-start | bytes 73736 | tf_op jit(solution)/shard_map/ppermute | solution.py:63
  77.0 25.4 %collective-permute-start.1 = (f32[3,8,256]{1,0,2:T(4,128)S(1)}, f32[3,8,256]{1,0,2:T(4,128)S(1)}, u32[]{:S(2)}, u32[]{:S(2)}) collective-permute-start(f32[3,8,256]{1,0,2:T(4,128)S(1)} %add.15), channel_id=1, source_target_pairs={{0,16},{8,24},{16,0},{24,8},{1,17},{9,25},{17,1},{25,9},{2,18},{10... | collective-permute-start | bytes 73736 | tf_op jit(solution)/shard_map/ppermute | solution.py:63
